TPU v7x, 512 devices: a whole 4x8x8 slice. The times are simulated.
512 devices in a mesh: row: 8 (over y), col: 64 (over z, x, core).
Axes of the slice: x: 4, y: 8, z: 8, core: 2. Of those that a mesh axis runs over, the one named last changes fastest.
Arguments:
- eigen_slab: float32 [8192, 65536], P('row', 'col'), may hold values from -6 to 6
- secular_poles: float32 [131072], P('col'), may hold values from 0 to 4, as said below
- coupling: float32 [131072], P('col'), may hold values from -7 to 7
- window_roots: float32 [128], replicated, may hold values from 0 to 4, as said below
- deflated: int32 [131072], P('col'), may hold values 0 or 1
- column_map: int32 [131072], P('col'), may hold values from 0 to 131071, as said below
Outputs:
- vectors: float32 [8192, 128], P(('row', 'col'))
Inputs may be any that keep to these rules, and one draw needn't show every extreme that they name: `column_map`: A permutation of the 131072 columns. Grid column c holds columns c * 1024 to (c + 1) * 1024 - 1 and 65536 + c * 1024 to 65536 + (c + 1) * 1024 - 1 of the slab, and positions c * 2048 to (c + 1) * 2048 - 1. Of one grid column's positions, exactly 64 map to the columns of one grid column, 32 to each of 62 others, none to the remaining one. `secular_poles`: each pole lies between (k + 0.2) * 4 / 256 and (k + 0.8) * 4 / 256 for a whole number k. `window_roots`: each root lies within 0.15 * 4 / 256 of k * 4 / 256 for a whole number k of 1 to 255.
All inputs are finite; a program needn't handle non-finite values. No bound on the sum of `deflated` on one device may be relied on, other than what follows from the above.
Results may differ from a plain program's by a relative error of at most 0.0003.
Values sent between devices are 32-bit elements; how exact they have to be, the bound alone decides.
A program may use at most 64 MiB of HBM per device.

v0:
```python
import jax
import jax.numpy as jnp
from jax import lax
from jax.sharding import PartitionSpec as P


def slot_plan(column_map, groups, cols_dev, capacity):
    block_len = column_map.shape[0]
    half_order = cols_dev * groups
    within = column_map % half_order
    target = within // cols_dev
    target_local = within % cols_dev + jnp.where(column_map >= half_order, cols_dev, 0)
    onehot = (target[:, None] == jnp.arange(groups, dtype=jnp.int32)[None, :]).astype(jnp.int32)
    slot_rank = jnp.sum(jnp.cumsum(onehot, axis=0) * onehot, axis=1) - 1
    slot_index = target * capacity + slot_rank
    sentinel = jnp.full((groups * capacity,), block_len, jnp.int32)
    slot_source = sentinel.at[slot_index].set(jnp.arange(block_len, dtype=jnp.int32))
    slot_target = sentinel.at[slot_index].set(target_local)
    return (slot_source, slot_target)


def route_rows(scaled, column_map, groups, cols_dev, capacity):
    slot_source, slot_target = slot_plan(column_map, groups, cols_dev, capacity)
    outgoing = jnp.take(scaled, slot_source, axis=0, mode="fill", fill_value=0.0)
    outgoing = outgoing.reshape(groups, capacity, scaled.shape[1])
    arrived, arrived_index = (
        lax.all_to_all(outgoing, "col", split_axis=0, concat_axis=0, tiled=True),
        lax.all_to_all(
            slot_target.reshape(groups, capacity), "col", split_axis=0, concat_axis=0, tiled=True
        ),
    )
    flat_rows = arrived.reshape(groups * capacity, scaled.shape[1])
    return jnp.zeros_like(scaled).at[arrived_index.reshape(-1)].set(flat_rows, mode="drop")


def body(eigen_slab, secular_poles, coupling, window_roots, deflated, column_map):
    groups = lax.axis_size("col")
    row_groups = lax.axis_size("row")
    block_len = secular_poles.shape[0]
    cols_dev = eigen_slab.shape[1]
    capacity = 2 * (block_len // groups)
    distance = secular_poles[:, None] - window_roots[None, :]
    entries = jnp.where(
        deflated[:, None] == 0, coupling[:, None] / distance, jnp.zeros_like(distance)
    )
    sum_squares = lax.psum(jnp.sum(entries * entries, axis=0), "col")
    inverse = lax.rsqrt(sum_squares)
    scaled = entries * inverse[None, :]
    placed = route_rows(scaled, column_map, groups, cols_dev, capacity)
    half_start = jnp.where(lax.axis_index("row") < row_groups // 2, 0, cols_dev)
    half_window = lax.dynamic_slice_in_dim(placed, half_start, cols_dev, 0)
    return lax.psum_scatter(
        jnp.dot(
            eigen_slab,
            half_window,
            precision=lax.Precision.HIGHEST,
            preferred_element_type=jnp.float32,
        ),
        "col",
        scatter_dimension=0,
        tiled=True,
    )


def solution(mesh):
    return jax.shard_map(
        body,
        mesh=mesh,
        in_specs=(P("row", "col"), P("col"), P("col"), P(), P("col"), P("col")),
        out_specs=P(("row", "col"), None),
        check_vma=False,
    )
```

profile of v0, /device:TPU:1, one launch (start us, length us, event | category | flops | bytes accessed | tf_op | source)
XLA Modules:
  0.0 473.3 jit_solution(13782609337282554614)
XLA Ops:
  6.5 0.7 fusion.9
  7.3 18.1 %reduce-window.6 = s32[64,16,128]{2,1,0:T(8,128)S(1)} reduce-window(s32[64,16,128]{2,1,0:T(8,128)S(1)} %fusion.6, s32[]{:T(128)} %constant.68.clone.1), window={size=1x1x128 pad=0_0x0_0x127_0}, to_apply=%region_0.1 | reduce-window | flops 16646144 | bytes 1048580 | tf_op jit(solution)/shard_map/reduce-window
  25.5 0.2 slice.10
  25.7 0.4 copy.14
  26.3 0.2 broadcast_add_fusion
  26.7 8.1 %scatter_custom_fusion = s32[4096]{0:T(1024)S(1)} fusion(s32[2048]{0:T(1024)S(1)} %compare_select_fusion.2, s32[2048]{0:T(1024)S(1)} %get-tuple-element.5, s32[]{:T(128)} %constant.67.clone.1), kind=kCustom, calls=%fused_computation.37 | custom fusion | bytes 16388 | tf_op jit(solution)/shard_map/scatter | solution.py:18
  34.8 0.7 all_to_all.9
  35.5 14.8 %all-to-all-start = ((s32[64,1,64]{2,1,0:T(1,128)}), s32[64,1,64]{2,1,0:T(1,128)S(1)}, u32[]{:S(2)}, u32[]{:S(2)}) async-start(s32[64,1,64]{2,1,0:T(1,128)} %all_to_all.9), calls=%async_computation | async-start | bytes 65536 | tf_op jit(solution)/shard_map/all_to_all | solution.py:28
  50.3 8.1 %scatter_custom_fusion.1 = s32[4096]{0:T(1024)S(1)} fusion(s32[2048]{0:T(1024)S(1)} %compare_select_fusion.2, s32[2048]{0:T(1024)S(1)} %iota.11, s32[]{:T(128)} %constant.67.clone.1), kind=kCustom, calls=%fused_computation.35 | custom fusion | bytes 16388 | tf_op jit(solution)/shard_map/scatter | solution.py:17
  58.5 1.0 multiply_reduce_fusion
  59.5 124.1 %psum.7 = f32[128]{0:T(128)S(1)} all-reduce(f32[128]{0:T(128)S(1)} %multiply_reduce_fusion), channel_id=1, replica_groups=mesh['row'=8,'col'=64] {'col'}, use_global_device_ids=true, to_apply=%region_6.7 | all-reduce | flops 128 | bytes 1024 | tf_op jit(solution)/shard_map/psum | solution.py:46
  183.6 0.9 fusion
  184.6 10.8 %gather_fusion = f32[4096,128]{1,0:T(8,128)S(1)} fusion(f32[2048,128]{1,0:T(8,128)S(1)} %fusion, s32[4096]{0:T(1024)S(1)} %fusion.7), kind=kCustom, calls=%fused_computation | custom fusion | bytes 4210688 | tf_op jit(solution)/shard_map/jit(_take)/gather | solution.py:24
  195.4 1.7 broadcast_select_fusion
  197.1 10.2 %all-to-all-start.1 = ((f32[64,64,128]{2,1,0:T(8,128)}), f32[64,64,128]{2,1,0:T(8,128)S(1)}, u32[]{:S(2)}, u32[]{:S(2)}) async-start(f32[64,64,128]{2,1,0:T(8,128)} %broadcast_select_fusion), calls=%async_computation.1 | async-start | bytes 4194304 | tf_op jit(solution)/shard_map/all_to_all | solution.py:27
  207.4 0.5 broadcast.104
  207.9 0.7 reduce.3
  208.7 48.3 %all-to-all-done.1 = f32[64,64,128]{2,1,0:T(8,128)S(1)} async-done(((f32[64,64,128]{2,1,0:T(8,128)}), f32[64,64,128]{2,1,0:T(8,128)S(1)}, u32[]{:S(2)}, u32[]{:S(2)}) %all-to-all-start.1) | async-done | bytes 2097184 | tf_op jit(solution)/shard_map/all_to_all | solution.py:27
  257.0 11.0 %scatter_custom_fusion.2 = f32[2048,128]{1,0:T(8,128)S(1)} fusion(s32[4096]{0:T(1024)S(1)} %bitcast.32, f32[4096,128]{1,0:T(8,128)S(1)} %bitcast.27, f32[]{:T(128)} %constant.66.clone.1), kind=kCustom, calls=%fused_computation.15 | custom fusion | bytes 1048580 | tf_op jit(solution)/shard_map/scatter | solution.py:33
  268.0 7.5 %convolution_bitcast_fusion = f32[1024,128]{0,1:T(8,128)} fusion(f32[1024,1024]{1,0:T(8,128)} %param.6, f32[2048,128]{1,0:T(8,128)S(1)} %scatter_custom_fusion.2, s32[]{:T(128)S(6)} %select_n.62), kind=kOutput, calls=%fused_computation.4 | convolution fusion | flops 1610612736 | bytes 5242884 | tf_op jit(solution)/shard_map/dot_general | solution.py:53
  275.6 1.3 dynamic-slice
  277.5 187.4 %all-reduce.3.cloned.1.call-done = f32[1024,128]{0,1:T(8,128)} async-done(((f32[1024,128]{0,1:T(8,128)}), f32[1024,128]{0,1:T(8,128)}) %all-reduce.3.cloned.1.call-update) | async-done | bytes 524304
  464.8 0.9 constant_dynamic-slice_fusion
  465.8 0.7 copy.13
  (23 shorter events, 0.7 us)
Async XLA Ops:
  7.3 51.2 %copy-start.2 = (s32[2048]{0:T(1024)S(1)}, s32[2048]{0:T(1024)}, u32[]{:S(2)}) copy-start(s32[2048]{0:T(1024)} %param.10) | copy-start | bytes 24580
  7.3 51.2 %copy-start = (f32[2048]{0:T(1024)S(1)}, f32[2048]{0:T(1024)}, u32[]{:S(2)}) copy-start(f32[2048]{0:T(1024)} %param.7) | copy-start | bytes 24580
  7.3 51.2 %copy-start.1 = (f32[2048]{0:T(1024)S(1)}, f32[2048]{0:T(1024)}, u32[]{:S(2)}) copy-start(f32[2048]{0:T(1024)} %param.8) | copy-start | bytes 24580
  7.3 51.2 %copy-start.3 = (f32[128]{0:T(128)S(1)}, f32[128]{0:T(128)}, u32[]{:S(2)}) copy-start(f32[128]{0:T(128)} %param.9) | copy-start | bytes 1540
  35.5 161.6 %all-to-all-start = ((s32[64,1,64]{2,1,0:T(1,128)}), s32[64,1,64]{2,1,0:T(1,128)S(1)}, u32[]{:S(2)}, u32[]{:S(2)}) async-start(s32[64,1,64]{2,1,0:T(1,128)} %all_to_all.9), calls=%async_computation | async-start | bytes 65536 | tf_op jit(solution)/shard_map/all_to_all | solution.py:28
  197.1 59.9 %all-to-all-start.1 = ((f32[64,64,128]{2,1,0:T(8,128)}), f32[64,64,128]{2,1,0:T(8,128)S(1)}, u32[]{:S(2)}, u32[]{:S(2)}) async-start(f32[64,64,128]{2,1,0:T(8,128)} %broadcast_select_fusion), calls=%async_computation.1 | async-start | bytes 4194304 | tf_op jit(solution)/shard_map/all_to_all | solution.py:27
  207.3 257.5 %all-reduce.3.cloned.1.call-start = ((), (), s32[]{:S(2)}) async-start(), calls=%async_computation.2 | async-start | bytes 1048576
Sparse Core Ops, SparseCore 0:
  275.7 189.1 all-reduce.2
where the time goes:
time: 475 us; the launch traced here: 473 us
  waiting for transfers between devices  236 us (50%)
  blocking collectives  124 us (26%)
  local copies, waits for them, and re-layouts  42.8 us (9%)
  starting transfers between devices  25.1 us (5%)
  other arithmetic  23.9 us (5%)
  between operations  14.3 us (3%)
  matrix products  7.48 us (2%)
    unnamed x2, waiting for transfers between devices  187 us
    psum x1, blocking collectives, body(): sum_squares = lax.psum(jnp.sum(entries * entries, axis=0), 'col')  124 us
    all_to_all x1, waiting for transfers between devices, route_rows(): lax.all_to_all(outgoing, 'col', split_axis=0, concat_axis=0, tiled=True)  48.3 us
    another operation x3, other arithmetic  18.5 us
    all_to_all x1, starting transfers between devices, route_rows(): lax.all_to_all(slot_target.reshape(groups, capacity), 'col', split_axis=0...  14.8 us
    scatter x1, local copies, waits for them, and re-layouts, route_rows(): jnp.zeros_like(scaled).at[arrived_index.reshape(-1)]  11 us
    gather x1, local copies, waits for them, and re-layouts, route_rows(): jnp.take(scaled, slot_source, axis=0, mode='fill', fill_value=0.0)  10.8 us
    all_to_all x1, starting transfers between devices, route_rows(): lax.all_to_all(outgoing, 'col', split_axis=0, concat_axis=0, tiled=True)  10.2 us
  transfers between devices with their start and end apart: 3, of which 2 were waited for; matrix products, arithmetic and copies ran while one was open for 5% of the time, Pallas kernels for 0%

commit v1 on v0

v1 whole, which is shorter than its diff:
```python
import jax
import jax.numpy as jnp
from jax import lax
from jax.experimental import pallas as pl
from jax.experimental.pallas import tpu as pltpu
from jax.sharding import PartitionSpec as P

MESH = pl.DeviceIdType.MESH
BF = jnp.bfloat16
F32 = jnp.float32
NT = (((1,), (1,)), ((), ()))
HALF = 65536
ORDER_X = (2, 1, 3, 0)


def dot_nt(a, b):
    return lax.dot_general(a, b, NT, preferred_element_type=F32)


def split3(v):
    hi = v.astype(BF)
    rest = v - hi.astype(F32)
    mid = rest.astype(BF)
    low = (rest - mid.astype(F32)).astype(BF)
    return hi.astype(F32), mid.astype(F32), low.astype(F32)


def kernel(
    slab, poles_in, coup_in, roots_in, defl_in, cmap_in, out_ref,
    sf, sh, sl, poles, coup, roots, defl, cmap,
    pieces, hots, slots, outgoing, recv_a, send_b, recv_b,
    place_l, place_r, entry, prod, recv_c, send_x, recv_x, send_z, recv_z,
    in_sem, slab_sem, sa, ra, sb, rb, sc, rc, sx, rx, sz, rz,
):
    row = lax.axis_index("row")
    col = lax.axis_index("col")
    z = col // 8
    g = col % 8
    x = g // 2
    core = g % 2

    smalls = [
        pltpu.make_async_copy(s, d, in_sem.at[i])
        for i, (s, d) in enumerate(
            [(cmap_in, cmap), (poles_in, poles), (coup_in, coup), (defl_in, defl), (roots_in, roots)]
        )
    ]
    for c in smalls:
        c.start()
    slabs = [
        pltpu.make_async_copy(slab.at[:, i // 2, i % 2], sf.at[i], slab_sem.at[i]) for i in range(8)
    ]
    for c in slabs:
        c.start()

    barrier = pltpu.get_barrier_semaphore()
    for k in range(1, 8):
        pl.semaphore_signal(barrier, inc=1, device_id=(row, z * 8 + (g + k) % 8), device_id_type=MESH)
        pl.semaphore_signal(barrier, inc=1, device_id=(row, ((z + k) % 8) * 8 + g), device_id_type=MESH)

    for c in smalls:
        c.wait()

    cm = cmap[...]
    upper = (cm >= HALF).astype(jnp.int32)
    within = cm - upper * HALF
    target = within >> 10
    local = within & 1023
    order = (target & 7) * 8 + (target >> 3)
    order = jnp.where(upper == row // 4, order, -1)
    pole_v = poles[...]
    coup_v = jnp.where(defl[...] == 0, coup[...], 0.0)
    coup[...] = coup_v
    vals = (
        *split3(pole_v),
        *split3(coup_v),
        (local >> 7).astype(F32),
        (local & 127).astype(F32),
    )
    dest_id = lax.broadcasted_iota(jnp.int32, (64, 128), 0)
    slot_id = (lax.broadcasted_iota(jnp.int32, (128, 128), 0) & 63).astype(F32)
    for b in range(16):
        hots[pl.ds(64 * b, 64), :] = (order[b:b + 1, :] == dest_id).astype(F32).astype(BF)
    before = lax.broadcasted_iota(jnp.int32, (128, 256), 0)
    at = lax.broadcasted_iota(jnp.int32, (128, 256), 1)
    tri = ((before < at) | (at >= 128)).astype(F32).astype(BF)
    counts = jnp.dot(hots[...], tri, preferred_element_type=F32)
    carry = jnp.zeros((64, 128), F32)
    for b in range(16):
        lanes = pl.ds(128 * b, 128)
        hot = hots[pl.ds(64 * b, 64), :]
        block = counts[64 * b:64 * b + 64]
        rank = jnp.sum(hot.astype(F32) * (block[:, :128] + carry), axis=0, keepdims=True)
        carry = carry + block[:, 128:]
        slots[:, lanes] = (rank == slot_id).astype(F32).astype(BF)
        for i, v in enumerate(vals):
            pieces[pl.ds(64 * i, 64), lanes] = hot * jnp.broadcast_to(v[b:b + 1, :], (64, 128)).astype(BF)
    routed = dot_nt(pieces[...], slots[...])
    pole_o = (routed[0:64] + routed[64:128]) + routed[128:192]
    coup_o = (routed[192:256] + routed[256:320]) + routed[320:384]
    at_o = routed[384:448] * 128.0 + routed[448:512]
    low_lane = lax.broadcasted_iota(jnp.int32, (64, 128), 1) < 64
    outgoing[:, 0] = jnp.where(low_lane, pole_o, coup_o).reshape(8, 8, 128)
    outgoing[:, 1] = at_o.reshape(8, 8, 128)

    pl.semaphore_wait(barrier, 14)
    copies_a = []
    for k in range(1, 8):
        to = (g + k) % 8
        c = pltpu.make_async_remote_copy(
            src_ref=outgoing.at[to], dst_ref=recv_a.at[g], send_sem=sa.at[k], recv_sem=ra.at[k],
            device_id=(row, z * 8 + to), device_id_type=MESH,
        )
        c.start()
        copies_a.append(c)
    recv_a[g] = outgoing[g]

    roots_t = jnp.transpose(jnp.broadcast_to(roots[...], (128, 128)))
    sums = jnp.zeros((128, 128), F32)
    for b in range(16):
        e = coup_v[b:b + 1, :] / (pole_v[b:b + 1, :] - roots_t)
        sums = sums + e * e
    sums = jnp.sum(jnp.transpose(sums), axis=0, keepdims=True)
    lane1 = lax.broadcasted_iota(jnp.int32, (8, 128), 1)
    sub1 = lax.broadcasted_iota(jnp.int32, (8, 128), 0)
    sums8 = jnp.broadcast_to(sums, (8, 128))
    sums8 = jnp.where(sub1 == 0, pltpu.roll(sums8, 64, 1), sums8)

    for c in copies_a:
        c.wait_recv()
    for s in range(8):
        for k in range(2):
            send_b[pl.ds(k * 8 + s, 8, stride=16), :] = recv_a[s, k]
    for t in range(8):
        rows = pl.ds(t * 16 + 8, 8)
        send_b[rows, :] = jnp.where(lane1 < 64, send_b[rows, :], sums8)
    copies_b = []
    for k in range(1, 8):
        to = (z + k) % 8
        c = pltpu.make_async_remote_copy(
            src_ref=send_b.at[pl.ds(pl.multiple_of(to * 16, 16), 16)],
            dst_ref=recv_b.at[pl.ds(pl.multiple_of(z * 16, 16), 16)],
            send_sem=sb.at[k], recv_sem=rb.at[k],
            device_id=(row, to * 8 + g), device_id_type=MESH,
        )
        c.start()
        copies_b.append(c)
    mine = pl.ds(pl.multiple_of(z * 16, 16), 16)
    recv_b[mine, :] = send_b[mine, :]

    for i in range(8):
        slabs[i].wait()

        @pl.loop(0, 8)
        def _(q):
            v = sf[i, q]
            hi = v.astype(BF)
            at16 = pl.ds(pl.multiple_of((i % 2) * 128 + q * 16, 16), 16)
            sh[i // 2, at16, :] = hi
            sl[i // 2, at16, :] = (v - hi.astype(F32)).astype(BF)

    for c in copies_b:
        c.wait_recv()

    val = jnp.concatenate([recv_b[pl.ds(16 * s, 8), :] for s in range(8)], axis=0)
    loc = jnp.concatenate([recv_b[pl.ds(16 * s + 8, 8), :] for s in range(8)], axis=0)
    low32 = lax.broadcasted_iota(jnp.int32, (32, 128), 1) < 64
    pole_r = jnp.where(low32, val[:32], pltpu.roll(val[32:], 64, 1))
    coup_r = jnp.where(low32, pltpu.roll(val[:32], 64, 1), val[32:])
    loc_r = jnp.where(low32, loc[:32], pltpu.roll(loc[32:], 64, 1)).astype(jnp.int32)
    loc_h = loc_r >> 7
    loc_l = loc_r & 127
    parts = (*split3(pole_r), *split3(coup_r))
    id128 = lax.broadcasted_iota(jnp.int32, (128, 128), 0)
    id8 = lax.broadcasted_iota(jnp.int32, (8, 128), 0)
    for b in range(32):
        lanes = pl.ds(128 * b, 128)
        place_l[:, lanes] = (loc_l[b:b + 1, :] == id128).astype(F32).astype(BF)
        hit = loc_h[b:b + 1, :] == id8
        place_r[:, lanes] = jnp.concatenate(
            [jnp.where(hit, v[b:b + 1, :], 0.0) for v in parts], axis=0
        ).astype(BF)
    placed = dot_nt(place_r[...], place_l[...])
    pole_p = (placed[0:8] + placed[8:16]) + placed[16:24]
    coup_p = (placed[24:32] + placed[32:40]) + placed[40:48]
    for h in range(8):
        e = coup_p[h:h + 1, :] / (pole_p[h:h + 1, :] - roots_t)
        hi = e.astype(BF)
        lanes = pl.ds(128 * h, 128)
        entry[pl.ds(0, 128), lanes] = hi
        entry[pl.ds(128, 128), lanes] = (e - hi.astype(F32)).astype(BF)

    tot = jnp.sum(jnp.concatenate([recv_b[pl.ds(16 * s + 8, 8), :].reshape(1, 8, 128) for s in range(8)], axis=0), axis=0)
    tot_row = jnp.where(lane1[:1] < 64, pltpu.roll(tot, 64, 1)[0:1], tot[1:2])
    tot8 = jnp.broadcast_to(tot_row, (8, 128))

    copies_c = {}
    copies_x = {}

    def pass_x(o):
        copies_c[o].wait_recv()
        send_x[o] = prod[o, core] + recv_c[o]
        if o:
            to = (x + o) % 4
            c = pltpu.make_async_remote_copy(
                src_ref=send_x.at[o], dst_ref=recv_x.at[o], send_sem=sx.at[o], recv_sem=rx.at[o],
                device_id=(row, z * 8 + to * 2 + core), device_id_type=MESH,
            )
            c.start()
            copies_x[o] = c

    last = None
    for o in ORDER_X:
        xp = (x + o) % 4
        r1 = dot_nt(sh[xp], entry[...])
        r2 = dot_nt(sl[xp], entry[pl.ds(0, 128), :])
        p = (r1[:, 128:] + r2) + r1[:, :128]
        prod[o, :, pl.ds(0, 128), :] = p.reshape(2, 128, 128)
        prod[o, :, pl.ds(128, 8), :] = jnp.broadcast_to(tot8.reshape(1, 8, 128), (2, 8, 128))
        c = pltpu.make_async_remote_copy(
            src_ref=prod.at[o, 1 - core], dst_ref=recv_c.at[o], send_sem=sc.at[o], recv_sem=rc.at[o],
            device_id=(row, z * 8 + x * 2 + (1 - core)), device_id_type=MESH,
        )
        c.start()
        copies_c[o] = c
        if last is not None:
            pass_x(last)
        last = o
    pass_x(last)
    total = send_x[0]
    for o in (1, 3, 2):
        copies_x[o].wait_recv()
        total = total + recv_x[o]
    send_z[...] = total[:128].reshape(8, 16, 128)
    scale = lax.rsqrt(total[128:129])
    copies_z = []
    for k in range(1, 8):
        to = (z + k) % 8
        c = pltpu.make_async_remote_copy(
            src_ref=send_z.at[to], dst_ref=recv_z.at[k], send_sem=sz.at[k], recv_sem=rz.at[k],
            device_id=(row, to * 8 + g), device_id_type=MESH,
        )
        c.start()
        copies_z.append(c)
    final = send_z[z]
    for k, c in enumerate(copies_z):
        c.wait_recv()
        final = final + recv_z[k + 1]
    out_ref[...] = final * scale
    for c in copies_a + copies_b + list(copies_c.values()) + list(copies_x.values()) + copies_z:
        c.wait_send()


def body(eigen_slab, secular_poles, coupling, window_roots, deflated, column_map):
    hbm = pl.BlockSpec(memory_space=pl.ANY)
    dma = pltpu.SemaphoreType.DMA
    return pl.pallas_call(
        kernel,
        out_shape=jax.ShapeDtypeStruct((16, 128), F32),
        in_specs=[hbm] * 6,
        out_specs=pl.BlockSpec(memory_space=pltpu.VMEM),
        scratch_shapes=[
            pltpu.VMEM((8, 8, 16, 1024), F32),
            pltpu.VMEM((4, 256, 1024), BF),
            pltpu.VMEM((4, 256, 1024), BF),
            pltpu.VMEM((16, 128), F32),
            pltpu.VMEM((16, 128), F32),
            pltpu.VMEM((1, 128), F32),
            pltpu.VMEM((16, 128), jnp.int32),
            pltpu.VMEM((16, 128), jnp.int32),
            pltpu.VMEM((512, 2048), BF),
            pltpu.VMEM((1024, 128), BF),
            pltpu.VMEM((128, 2048), BF),
            pltpu.VMEM((8, 2, 8, 128), F32),
            pltpu.VMEM((8, 2, 8, 128), F32),
            pltpu.VMEM((128, 128), F32),
            pltpu.VMEM((128, 128), F32),
            pltpu.VMEM((128, 4096), BF),
            pltpu.VMEM((48, 4096), BF),
            pltpu.VMEM((256, 1024), BF),
            pltpu.VMEM((4, 2, 136, 128), F32),
            pltpu.VMEM((4, 136, 128), F32),
            pltpu.VMEM((4, 136, 128), F32),
            pltpu.VMEM((4, 136, 128), F32),
            pltpu.VMEM((8, 16, 128), F32),
            pltpu.VMEM((8, 16, 128), F32),
            dma((5,)), dma((8,)),
            dma((8,)), dma((8,)), dma((8,)), dma((8,)),
            dma((4,)), dma((4,)), dma((4,)), dma((4,)),
            dma((8,)), dma((8,)),
        ],
        compiler_params=pltpu.CompilerParams(
            collective_id=0, has_side_effects=True, vmem_limit_bytes=40 * 1024 * 1024
        ),
        name="top_merge",
    )(
        eigen_slab.reshape(8, 4, 2, 16, 1024),
        secular_poles.reshape(16, 128),
        coupling.reshape(16, 128),
        window_roots.reshape(1, 128),
        deflated.reshape(16, 128),
        column_map.reshape(16, 128),
    )


def solution(mesh):
    return jax.shard_map(
        body,
        mesh=mesh,
        in_specs=(P("row", "col"), P("col"), P("col"), P(), P("col"), P("col")),
        out_specs=P(("row", "col"), None),
        check_vma=False,
    )
```

time: 475 us -> 40.7 us (0.09)
  waiting for transfers between devices: 236 us -> 0 us
  blocking collectives: 124 us -> 0 us
  local copies, waits for them, and re-layouts: 42.8 us -> 6.23 us
  Pallas kernels: 0 us -> 34.1 us
  starting transfers between devices: 25.1 us -> 0 us
  other arithmetic: 23.9 us -> 0 us
  between operations: 14.3 us -> 0.02 us
  matrix products: 7.48 us -> 0 us
    unnamed x2 -> x0, waiting for transfers between devices: 187 us -> none
    psum x1 -> x0, blocking collectives: 124 us -> none  [body(): sum_squares = lax.psum(jnp.sum(entries * entries, axis=0), 'col')]
    all_to_all x2 -> x0, waiting for transfers between devices: 48.3 us -> none  [the longest x1 48.3 us: route_rows(): lax.all_to_all(outgoing, 'col', split_axis=0, concat_axis=0, tiled=True)]
    pallas_call x0 -> x1, Pallas kernels: none -> 34.1 us  [body(): pl.pallas_call(kernel, out_shape=jax.ShapeDtypeStruct((16, 128), F32), in...]
    scatter x3 -> x0, local copies, waits for them, and re-layouts: 27.2 us -> none  [the longest x1 11 us: route_rows(): jnp.zeros_like(scaled).at[arrived_index.reshape(-1)]]
    all_to_all x2 -> x0, starting transfers between devices: 25 us -> none  [the longest x1 14.8 us: route_rows(): lax.all_to_all(slot_target.reshape(groups, capacity), 'col', split_axis=0...]
    another operation x3 -> x0, other arithmetic: 18.5 us -> none
    gather x1 -> x0, local copies, waits for them, and re-layouts: 10.8 us -> none  [route_rows(): jnp.take(scaled, slot_source, axis=0, mode='fill', fill_value=0.0)]
  transfers between devices with their start and end apart: 3 -> 0, of which waited for: 2 -> 0; matrix products, arithmetic and copies ran while one was open for 5% -> 0% of each run, Pallas kernels for 0% -> 0%
where the time goes in v1:
time: 40.7 us; the launch traced here: 40.4 us
  Pallas kernels  34.1 us (84%)
  local copies, waits for them, and re-layouts  6.23 us (15%)
    pallas_call x1, Pallas kernels, body(): pl.pallas_call(kernel, out_shape=jax.ShapeDtypeStruct((16, 128), F32), in...  34.1 us
    unnamed x13, local copies, waits for them, and re-layouts  6.23 us

profile of v1, /device:TPU:1, one launch (start us, length us, event | category | flops | bytes accessed | tf_op | source)
XLA Modules:
  0.0 40.4 jit_solution(15418360465608744624)
XLA Ops:
  0.0 0.0 copy-start
  0.0 2.2 %copy-done = f32[1024,1024]{1,0:T(8,128)S(1)} copy-done((f32[1024,1024]{1,0:T(8,128)S(1)}, f32[1024,1024]{1,0:T(8,128)}, u32[]{:S(2)}) %copy-start) | copy-done | bytes 4194328
  2.2 0.0 copy-start.1
  2.2 0.7 %copy-done.1 = f32[2048]{0:T(1024)S(1)} copy-done((f32[2048]{0:T(1024)S(1)}, f32[2048]{0:T(1024)}, u32[]{:S(2)}) %copy-start.1) | copy-done | bytes 8216
  2.9 0.0 copy-start.2
  2.9 0.7 %copy-done.2 = f32[2048]{0:T(1024)S(1)} copy-done((f32[2048]{0:T(1024)S(1)}, f32[2048]{0:T(1024)}, u32[]{:S(2)}) %copy-start.2) | copy-done | bytes 8216
  3.6 0.0 copy-start.3
  3.6 0.7 %copy-done.3 = s32[2048]{0:T(1024)S(1)} copy-done((s32[2048]{0:T(1024)S(1)}, s32[2048]{0:T(1024)}, u32[]{:S(2)}) %copy-start.3) | copy-done | bytes 8216
  4.3 0.0 copy-start.4
  4.3 0.7 %copy-done.4 = s32[2048]{0:T(1024)S(1)} copy-done((s32[2048]{0:T(1024)S(1)}, s32[2048]{0:T(1024)}, u32[]{:S(2)}) %copy-start.4) | copy-done | bytes 8216
  5.0 0.0 copy-start.5
  5.0 0.7 %copy-done.5 = f32[128]{0:T(128)S(1)} copy-done((f32[128]{0:T(128)S(1)}, f32[128]{0:T(128)}, u32[]{:S(2)}) %copy-start.5) | copy-done | bytes 536
  5.6 34.1 %top_merge.1 = f32[16,128]{1,0:T(8,128)S(1)} custom-call(f32[8,4,2,16,1024]{4,3,2,1,0:T(8,128)S(1)} %bitcast.6, f32[16,128]{1,0:T(8,128)S(1)} %bitcast.7, f32[16,128]{1,0:T(8,128)S(1)} %bitcast.8, f32[1,128]{1,0:T(1,128)S(1)} %bitcast.11, s32[16,128]{1,0:T(8,128)S(1)} %bitcast.9, s32[16,128]{1,0:T(8,128)S(1)} %bitcast.10), custom_call_target="tpu_custom_call" | custom-call | tf_op jit(solution)/shard_map/top_merge/pallas_call | solution.py:257
  39.8 0.6 %copy.8 = f32[16,128]{1,0:T(8,128)} copy(f32[16,128]{1,0:T(8,128)S(1)} %top_merge.1) | data formatting | bytes 16384
Async XLA Ops:
  0.0 2.2 %copy-start = (f32[1024,1024]{1,0:T(8,128)S(1)}, f32[1024,1024]{1,0:T(8,128)}, u32[]{:S(2)}) copy-start(f32[1024,1024]{1,0:T(8,128)} %param.6) | copy-start | bytes 12582916
  2.2 0.7 %copy-start.1 = (f32[2048]{0:T(1024)S(1)}, f32[2048]{0:T(1024)}, u32[]{:S(2)}) copy-start(f32[2048]{0:T(1024)} %param.7) | copy-start | bytes 24580
  2.9 0.7 %copy-start.2 = (f32[2048]{0:T(1024)S(1)}, f32[2048]{0:T(1024)}, u32[]{:S(2)}) copy-start(f32[2048]{0:T(1024)} %param.8) | copy-start | bytes 24580
  3.6 0.7 %copy-start.3 = (s32[2048]{0:T(1024)S(1)}, s32[2048]{0:T(1024)}, u32[]{:S(2)}) copy-start(s32[2048]{0:T(1024)} %param.10) | copy-start | bytes 24580
  4.3 0.7 %copy-start.4 = (s32[2048]{0:T(1024)S(1)}, s32[2048]{0:T(1024)}, u32[]{:S(2)}) copy-start(s32[2048]{0:T(1024)} %param.11) | copy-start | bytes 24580
  5.0 0.7 %copy-start.5 = (f32[128]{0:T(128)S(1)}, f32[128]{0:T(128)}, u32[]{:S(2)}) copy-start(f32[128]{0:T(128)} %param.9) | copy-start | bytes 1540

commit v2 on v1

--- a/solution.py
+++ b/solution.py
@@ -39,6 +39,11 @@
     x = g // 2
     core = g % 2
 
+    barrier = pltpu.get_barrier_semaphore()
+    for k in range(1, 8):
+        pl.semaphore_signal(barrier, inc=1, device_id=(row, z * 8 + (g + k) % 8), device_id_type=MESH)
+        pl.semaphore_signal(barrier, inc=1, device_id=(row, ((z + k) % 8) * 8 + g), device_id_type=MESH)
+
     smalls = [
         pltpu.make_async_copy(s, d, in_sem.at[i])
         for i, (s, d) in enumerate(
@@ -52,11 +57,6 @@
     ]
     for c in slabs:
         c.start()
-
-    barrier = pltpu.get_barrier_semaphore()
-    for k in range(1, 8):
-        pl.semaphore_signal(barrier, inc=1, device_id=(row, z * 8 + (g + k) % 8), device_id_type=MESH)
-        pl.semaphore_signal(barrier, inc=1, device_id=(row, ((z + k) % 8) * 8 + g), device_id_type=MESH)
 
     for c in smalls:
         c.wait()
@@ -252,7 +252,7 @@
 
 
 def body(eigen_slab, secular_poles, coupling, window_roots, deflated, column_map):
-    hbm = pl.BlockSpec(memory_space=pl.ANY)
+    hbm = pl.BlockSpec(memory_space=pltpu.HBM)
     dma = pltpu.SemaphoreType.DMA
     return pl.pallas_call(
         kernel,
@@ -294,12 +294,17 @@
         ),
         name="top_merge",
     )(
-        eigen_slab.reshape(8, 4, 2, 16, 1024),
-        secular_poles.reshape(16, 128),
-        coupling.reshape(16, 128),
-        window_roots.reshape(1, 128),
-        deflated.reshape(16, 128),
-        column_map.reshape(16, 128),
+        *(
+            pltpu.with_memory_space_constraint(v, pltpu.HBM)
+            for v in (
+                eigen_slab.reshape(8, 4, 2, 16, 1024),
+                secular_poles.reshape(16, 128),
+                coupling.reshape(16, 128),
+                window_roots.reshape(1, 128),
+                deflated.reshape(16, 128),
+                column_map.reshape(16, 128),
+            )
+        )
     )
 
 

time: 40.7 us -> 34.5 us (0.85)
  local copies, waits for them, and re-layouts: 6.23 us -> 0.6 us
    unnamed x13 -> x1, local copies, waits for them, and re-layouts: 6.23 us -> 0.6 us
where the time goes in v2:
time: 34.5 us; the launch traced here: 34.4 us
  Pallas kernels  33.8 us (98%)
  local copies, waits for them, and re-layouts  0.6 us (2%)
    pallas_call x1, Pallas kernels, body(): pl.pallas_call(kernel, out_shape=jax.ShapeDtypeStruct((16, 128), F32), in...  33.8 us

profile of v2, /device:TPU:1, one launch (start us, length us, event | category | flops | bytes accessed | tf_op | source)
XLA Modules:
  0.0 34.4 jit_solution(3333914082789239706)
XLA Ops:
  0.0 33.8 %top_merge.1 = f32[16,128]{1,0:T(8,128)S(1)} custom-call(f32[8,4,2,16,1024]{4,3,2,1,0:T(8,128)} %bitcast.6, f32[16,128]{1,0:T(8,128)} %bitcast.7, f32[16,128]{1,0:T(8,128)} %bitcast.8, f32[1,128]{1,0:T(1,128)} %bitcast.11, s32[16,128]{1,0:T(8,128)} %bitcast.9, s32[16,128]{1,0:T(8,128)} %bitcast.10), custom_call_target="tpu_custom_call" | custom-call | tf_op jit(solution)/shard_map/top_merge/pallas_call | solution.py:257
  33.8 0.6 %copy.8 = f32[16,128]{1,0:T(8,128)} copy(f32[16,128]{1,0:T(8,128)S(1)} %top_merge.1) | data formatting | bytes 16384

commit v3 on v2

v3 whole, which is shorter than its diff:
```python
import jax
import jax.numpy as jnp
from jax import lax
from jax.experimental import pallas as pl
from jax.experimental.pallas import tpu as pltpu
from jax.sharding import PartitionSpec as P

MESH = pl.DeviceIdType.MESH
BF = jnp.bfloat16
F32 = jnp.float32
NT = (((1,), (1,)), ((), ()))
HALF = 65536
STEPS_Z = (4, 3, 5, 2, 6, 1, 7, 0)
STEPS_X = (2, 1, 3, 0)


def dot_nt(a, b):
    return lax.dot_general(a, b, NT, preferred_element_type=F32)


def split3(v):
    hi = v.astype(BF)
    rest = v - hi.astype(F32)
    mid = rest.astype(BF)
    low = (rest - mid.astype(F32)).astype(BF)
    return hi.astype(F32), mid.astype(F32), low.astype(F32)


def kernel(
    slab, poles_in, coup_in, roots_in, defl_in, cmap_in, out_ref,
    sf, sh, sl, poles, coup, roots, defl, cmap,
    pieces, hots, slots, outgoing, recv_a, recv_b, pass_b,
    place_l, place_r, entry, prod, recv_c, send_r, recv_r,
    in_sem, slab_sem, sa, ra, sb, rb, sc, rc, sr, rr,
):
    row = lax.axis_index("row")
    col = lax.axis_index("col")
    chip = col // 2
    z = chip // 4
    x = chip % 4
    core = col % 2
    sibling = (row, chip * 2 + (1 - core))
    others = [
        ((z + dz) % 8 * 4 + (x + dx) % 4) for dz in STEPS_Z for dx in STEPS_X if dz or dx
    ]

    barrier = pltpu.get_barrier_semaphore()
    for to in others:
        pl.semaphore_signal(barrier, inc=1, device_id=(row, to * 2 + core), device_id_type=MESH)
    pl.semaphore_signal(barrier, inc=1, device_id=sibling, device_id_type=MESH)

    smalls = [
        pltpu.make_async_copy(s, d, in_sem.at[i])
        for i, (s, d) in enumerate(
            [(cmap_in, cmap), (poles_in, poles), (coup_in, coup), (defl_in, defl), (roots_in, roots)]
        )
    ]
    for c in smalls:
        c.start()
    slabs = [
        pltpu.make_async_copy(slab.at[pl.ds(i // 2 * 2, 2), :, i % 2], sf.at[i], slab_sem.at[i]) for i in range(8)
    ]
    for c in slabs:
        c.start()

    for c in smalls:
        c.wait()

    cm = cmap[...]
    upper = (cm >= HALF).astype(jnp.int32)
    within = cm - upper * HALF
    target = within >> 10
    local = within & 1023
    order = (target & 1) * 32 + (target >> 1)
    order = jnp.where(upper == row // 4, order, -1)
    pole_v = poles[...]
    coup_v = jnp.where(defl[...] == 0, coup[...], 0.0)
    vals = (
        *split3(pole_v),
        *split3(coup_v),
        (local >> 7).astype(F32),
        (local & 127).astype(F32),
    )
    dest_id = lax.broadcasted_iota(jnp.int32, (64, 128), 0)
    slot_id = (lax.broadcasted_iota(jnp.int32, (128, 128), 0) & 63).astype(F32)
    for b in range(16):
        hots[pl.ds(64 * b, 64), :] = (order[b:b + 1, :] == dest_id).astype(F32).astype(BF)
    before = lax.broadcasted_iota(jnp.int32, (128, 256), 0)
    at = lax.broadcasted_iota(jnp.int32, (128, 256), 1)
    tri = ((before < at) | (at >= 128)).astype(F32).astype(BF)
    counts = jnp.dot(hots[...], tri, preferred_element_type=F32)
    carry = jnp.zeros((64, 128), F32)
    for b in range(16):
        lanes = pl.ds(128 * b, 128)
        hot = hots[pl.ds(64 * b, 64), :]
        block = counts[64 * b:64 * b + 64]
        rank = jnp.sum(hot.astype(F32) * (block[:, :128] + carry), axis=0, keepdims=True)
        carry = carry + block[:, 128:]
        slots[:, lanes] = (rank == slot_id).astype(F32).astype(BF)
        for i, v in enumerate(vals):
            pieces[pl.ds(64 * i, 64), lanes] = hot * jnp.broadcast_to(v[b:b + 1, :], (64, 128)).astype(BF)
    routed = dot_nt(pieces[...], slots[...])
    pole_o = (routed[0:64] + routed[64:128]) + routed[128:192]
    coup_o = (routed[192:256] + routed[256:320]) + routed[320:384]
    at_o = routed[384:448] * 128.0 + routed[448:512]
    roots_t = jnp.transpose(jnp.broadcast_to(roots[...], (128, 128)))
    sums = jnp.zeros((128, 128), F32)
    for b in range(16):
        e = coup_v[b:b + 1, :] / (pole_v[b:b + 1, :] - roots_t)
        sums = sums + e * e
    sums = jnp.sum(jnp.transpose(sums), axis=0, keepdims=True)
    low_lane = lax.broadcasted_iota(jnp.int32, (32, 128), 1) < 64
    for i, v in enumerate((pole_o, coup_o, at_o)):
        outgoing[i] = jnp.where(low_lane, v[:32], v[32:])
    outgoing[3] = jnp.broadcast_to(sums, (32, 128))

    pl.semaphore_wait(barrier, 32)
    copies_a = []
    for k, to in enumerate(others):
        c = pltpu.make_async_remote_copy(
            src_ref=outgoing.at[:, pl.ds(to, 1)], dst_ref=recv_a.at[:, pl.ds(chip, 1)],
            send_sem=sa.at[k], recv_sem=ra.at[k],
            device_id=(row, to * 2 + core), device_id_type=MESH,
        )
        c.start()
        copies_a.append(c)

    for i in range(8):
        slabs[i].wait()

        @pl.loop(0, 8)
        def _(q):
            v = sf[i, q // 4, q % 4]
            hi = v.astype(BF)
            at16 = pl.ds(pl.multiple_of((i % 2) * 128 + q * 16, 16), 16)
            sh[i // 2, at16, :] = hi
            sl[i // 2, at16, :] = (v - hi.astype(F32)).astype(BF)

    for c in copies_a:
        c.wait_recv()
    here = lax.broadcasted_iota(jnp.int32, (32, 128), 0) == chip
    for i in range(4):
        v = jnp.where(here, outgoing[i], recv_a[i])
        pass_b[i] = v if i < 3 else jnp.broadcast_to(jnp.sum(v, axis=0, keepdims=True), (32, 128))
    pair = pltpu.make_async_remote_copy(
        src_ref=pass_b, dst_ref=recv_b, send_sem=sb.at[0], recv_sem=rb.at[0],
        device_id=sibling, device_id_type=MESH,
    )
    pair.start()
    pair.wait_recv()

    own_lane = (lax.broadcasted_iota(jnp.int32, (32, 128), 1) >> 6) == core
    pole_r, coup_r, loc_r = (
        jnp.where(own_lane, pass_b[i], pltpu.roll(recv_b[i], 64, 1)) for i in range(3)
    )
    scale = lax.rsqrt(pass_b[3, 0:1, :] + recv_b[3, 0:1, :])
    loc_r = loc_r.astype(jnp.int32)
    loc_h = loc_r >> 7
    loc_l = loc_r & 127
    parts = (*split3(pole_r), *split3(coup_r))
    id128 = lax.broadcasted_iota(jnp.int32, (128, 128), 0)
    id8 = lax.broadcasted_iota(jnp.int32, (8, 128), 0)
    for b in range(32):
        lanes = pl.ds(128 * b, 128)
        place_l[:, lanes] = (loc_l[b:b + 1, :] == id128).astype(F32).astype(BF)
        hit = loc_h[b:b + 1, :] == id8
        place_r[:, lanes] = jnp.concatenate(
            [jnp.where(hit, v[b:b + 1, :], 0.0) for v in parts], axis=0
        ).astype(BF)
    placed = dot_nt(place_r[...], place_l[...])
    pole_p = (placed[0:8] + placed[8:16]) + placed[16:24]
    coup_p = (placed[24:32] + placed[32:40]) + placed[40:48]
    for h in range(8):
        e = coup_p[h:h + 1, :] / (pole_p[h:h + 1, :] - roots_t)
        hi = e.astype(BF)
        lanes = pl.ds(128 * h, 128)
        entry[pl.ds(0, 128), lanes] = hi
        entry[pl.ds(128, 128), lanes] = (e - hi.astype(F32)).astype(BF)

    copies_c = []
    copies_r = []

    def send_on(m):
        copies_c[m].wait_recv()
        send_r[pl.ds(8 * m, 8)] = (prod[m, core] + recv_c[m]).reshape(8, 16, 128)
        for i in range(8):
            to = (2 * m + i // 4) * 4 + (x + STEPS_X[i % 4]) % 4

            @pl.when(to != chip)
            def _():
                remote(to).start()

    def remote(to):
        return pltpu.make_async_remote_copy(
            src_ref=send_r.at[to], dst_ref=recv_r.at[chip], send_sem=sr.at[to], recv_sem=rr.at[chip],
            device_id=(row, to * 2 + core), device_id_type=MESH,
        )

    for m in range(4):
        r1 = dot_nt(sh[m], entry[...])
        r2 = dot_nt(sl[m], entry[pl.ds(0, 128), :])
        p = (r1[:, 128:] + r2) + r1[:, :128]
        prod[m] = p.reshape(2, 128, 128)
        c = pltpu.make_async_remote_copy(
            src_ref=prod.at[m, 1 - core], dst_ref=recv_c.at[m], send_sem=sc.at[m], recv_sem=rc.at[m],
            device_id=sibling, device_id_type=MESH,
        )
        c.start()
        copies_c.append(c)
        if m:
            send_on(m - 1)
    send_on(3)
    final = send_r[chip]
    for to in others:
        pltpu.make_async_remote_copy(
            src_ref=send_r.at[to], dst_ref=recv_r.at[to], send_sem=sr.at[to], recv_sem=rr.at[to],
            device_id=(row, to * 2 + core), device_id_type=MESH,
        ).wait_recv()
        final = final + recv_r[to]
    out_ref[...] = final * scale
    for to in others:
        remote(to).wait_send()
    for c in [*copies_a, pair, *copies_c]:
        c.wait_send()


def body(eigen_slab, secular_poles, coupling, window_roots, deflated, column_map):
    hbm = pl.BlockSpec(memory_space=pltpu.HBM)
    dma = pltpu.SemaphoreType.DMA
    return pl.pallas_call(
        kernel,
        out_shape=jax.ShapeDtypeStruct((16, 128), F32),
        in_specs=[hbm] * 6,
        out_specs=pl.BlockSpec(memory_space=pltpu.VMEM),
        scratch_shapes=[
            pltpu.VMEM((8, 2, 4, 16, 1024), F32),
            pltpu.VMEM((4, 256, 1024), BF),
            pltpu.VMEM((4, 256, 1024), BF),
            pltpu.VMEM((16, 128), F32),
            pltpu.VMEM((16, 128), F32),
            pltpu.VMEM((1, 128), F32),
            pltpu.VMEM((16, 128), jnp.int32),
            pltpu.VMEM((16, 128), jnp.int32),
            pltpu.VMEM((512, 2048), BF),
            pltpu.VMEM((1024, 128), BF),
            pltpu.VMEM((128, 2048), BF),
            pltpu.VMEM((4, 32, 128), F32),
            pltpu.VMEM((4, 32, 128), F32),
            pltpu.VMEM((4, 32, 128), F32),
            pltpu.VMEM((4, 32, 128), F32),
            pltpu.VMEM((128, 4096), BF),
            pltpu.VMEM((48, 4096), BF),
            pltpu.VMEM((256, 1024), BF),
            pltpu.VMEM((4, 2, 128, 128), F32),
            pltpu.VMEM((4, 128, 128), F32),
            pltpu.VMEM((32, 16, 128), F32),
            pltpu.VMEM((32, 16, 128), F32),
            dma((5,)), dma((8,)),
            dma((31,)), dma((31,)), dma((1,)), dma((1,)),
            dma((4,)), dma((4,)), dma((32,)), dma((32,)),
        ],
        compiler_params=pltpu.CompilerParams(
            collective_id=0, has_side_effects=True, vmem_limit_bytes=40 * 1024 * 1024
        ),
        name="top_merge",
    )(
        *(
            pltpu.with_memory_space_constraint(v, pltpu.HBM)
            for v in (
                eigen_slab.reshape(8, 4, 2, 16, 1024),
                secular_poles.reshape(16, 128),
                coupling.reshape(16, 128),
                window_roots.reshape(1, 128),
                deflated.reshape(16, 128),
                column_map.reshape(16, 128),
            )
        )
    )


def solution(mesh):
    return jax.shard_map(
        body,
        mesh=mesh,
        in_specs=(P("row", "col"), P("col"), P("col"), P(), P("col"), P("col")),
        out_specs=P(("row", "col"), None),
        check_vma=False,
    )
```

time: 34.5 us -> 32.2 us (0.933)
  Pallas kernels: 33.8 us -> 31.4 us
    pallas_call x1, Pallas kernels: 33.8 us -> 31.4 us  [body(): pl.pallas_call(kernel, out_shape=jax.ShapeDtypeStruct((16, 128), F32), in...]
where the time goes in v3:
time: 32.2 us; the launch traced here: 32 us
  Pallas kernels  31.4 us (98%)
  local copies, waits for them, and re-layouts  0.6 us (2%)
    pallas_call x1, Pallas kernels, body(): pl.pallas_call(kernel, out_shape=jax.ShapeDtypeStruct((16, 128), F32), in...  31.4 us

profile of v3, /device:TPU:1, one launch (start us, length us, event | category | flops | bytes accessed | tf_op | source)
XLA Modules:
  0.0 32.0 jit_solution(13837432344180150243)
XLA Ops:
  0.0 31.4 %top_merge.1 = f32[16,128]{1,0:T(8,128)S(1)} custom-call(f32[8,4,2,16,1024]{4,3,2,1,0:T(8,128)} %bitcast.6, f32[16,128]{1,0:T(8,128)} %bitcast.7, f32[16,128]{1,0:T(8,128)} %bitcast.8, f32[1,128]{1,0:T(1,128)} %bitcast.11, s32[16,128]{1,0:T(8,128)} %bitcast.9, s32[16,128]{1,0:T(8,128)} %bitcast.10), custom_call_target="tpu_custom_call" | custom-call | tf_op jit(solution)/shard_map/top_merge/pallas_call | solution.py:230
  31.4 0.6 %copy.8 = f32[16,128]{1,0:T(8,128)} copy(f32[16,128]{1,0:T(8,128)S(1)} %top_merge.1) | data formatting | bytes 16384

commit v4 on v3

--- a/solution.py
+++ b/solution.py
@@ -41,24 +41,24 @@
     core = col % 2
     sibling = (row, chip * 2 + (1 - core))
     others = [
-        ((z + dz) % 8 * 4 + (x + dx) % 4) for dz in STEPS_Z for dx in STEPS_X if dz or dx
+        lax.rem(z + dz, 8) * 4 + lax.rem(x + dx, 4) for dz in STEPS_Z for dx in STEPS_X if dz or dx
     ]
 
+    smalls = [
+        pltpu.make_async_copy(s, d, in_sem.at[i])
+        for i, (s, d) in enumerate(
+            [(cmap_in, cmap), (poles_in, poles), (coup_in, coup), (defl_in, defl), (roots_in, roots)]
+        )
+    ]
+    for c in smalls:
+        c.start()
     barrier = pltpu.get_barrier_semaphore()
     for to in others:
         pl.semaphore_signal(barrier, inc=1, device_id=(row, to * 2 + core), device_id_type=MESH)
     pl.semaphore_signal(barrier, inc=1, device_id=sibling, device_id_type=MESH)
 
-    smalls = [
-        pltpu.make_async_copy(s, d, in_sem.at[i])
-        for i, (s, d) in enumerate(
-            [(cmap_in, cmap), (poles_in, poles), (coup_in, coup), (defl_in, defl), (roots_in, roots)]
-        )
-    ]
-    for c in smalls:
-        c.start()
     slabs = [
-        pltpu.make_async_copy(slab.at[pl.ds(i // 2 * 2, 2), :, i % 2], sf.at[i], slab_sem.at[i]) for i in range(8)
+        pltpu.make_async_copy(slab.at[pl.ds(2 * i, 2)], sf.at[i], slab_sem.at[i]) for i in range(4)
     ]
     for c in slabs:
         c.start()
@@ -115,35 +115,37 @@
     outgoing[3] = jnp.broadcast_to(sums, (32, 128))
 
     pl.semaphore_wait(barrier, 32)
-    copies_a = []
-    for k, to in enumerate(others):
+    for to in others:
         c = pltpu.make_async_remote_copy(
             src_ref=outgoing.at[:, pl.ds(to, 1)], dst_ref=recv_a.at[:, pl.ds(chip, 1)],
-            send_sem=sa.at[k], recv_sem=ra.at[k],
+            send_sem=sa, recv_sem=ra,
             device_id=(row, to * 2 + core), device_id_type=MESH,
         )
         c.start()
-        copies_a.append(c)
-
-    for i in range(8):
-        slabs[i].wait()
-
-        @pl.loop(0, 8)
-        def _(q):
-            v = sf[i, q // 4, q % 4]
-            hi = v.astype(BF)
-            at16 = pl.ds(pl.multiple_of((i % 2) * 128 + q * 16, 16), 16)
-            sh[i // 2, at16, :] = hi
-            sl[i // 2, at16, :] = (v - hi.astype(F32)).astype(BF)
-
-    for c in copies_a:
-        c.wait_recv()
+
+    for m in range(4):
+        slabs[m].wait()
+        for half in range(2):
+
+            @pl.loop(0, 8)
+            def _(q):
+                v = sf[m, q // 4, q % 4, half]
+                hi = v.astype(BF)
+                at16 = pl.ds(pl.multiple_of(half * 128 + q * 16, 16), 16)
+                sh[m, at16, :] = hi
+                sl[m, at16, :] = (v - hi.astype(F32)).astype(BF)
+
+    all_a = pltpu.make_async_remote_copy(
+        src_ref=outgoing.at[:, pl.ds(0, 31)], dst_ref=recv_a.at[:, pl.ds(0, 31)],
+        send_sem=sa, recv_sem=ra, device_id=sibling, device_id_type=MESH,
+    )
+    all_a.wait_recv()
     here = lax.broadcasted_iota(jnp.int32, (32, 128), 0) == chip
     for i in range(4):
         v = jnp.where(here, outgoing[i], recv_a[i])
         pass_b[i] = v if i < 3 else jnp.broadcast_to(jnp.sum(v, axis=0, keepdims=True), (32, 128))
     pair = pltpu.make_async_remote_copy(
-        src_ref=pass_b, dst_ref=recv_b, send_sem=sb.at[0], recv_sem=rb.at[0],
+        src_ref=pass_b, dst_ref=recv_b, send_sem=sb, recv_sem=rb,
         device_id=sibling, device_id_type=MESH,
     )
     pair.start()
@@ -184,7 +186,7 @@
         copies_c[m].wait_recv()
         send_r[pl.ds(8 * m, 8)] = (prod[m, core] + recv_c[m]).reshape(8, 16, 128)
         for i in range(8):
-            to = (2 * m + i // 4) * 4 + (x + STEPS_X[i % 4]) % 4
+            to = (2 * m + i // 4) * 4 + lax.rem(x + STEPS_X[i % 4], 4)
 
             @pl.when(to != chip)
             def _():
@@ -192,7 +194,7 @@
 
     def remote(to):
         return pltpu.make_async_remote_copy(
-            src_ref=send_r.at[to], dst_ref=recv_r.at[chip], send_sem=sr.at[to], recv_sem=rr.at[chip],
+            src_ref=send_r.at[to], dst_ref=recv_r.at[chip], send_sem=sr, recv_sem=rr,
             device_id=(row, to * 2 + core), device_id_type=MESH,
         )
 
@@ -210,17 +212,16 @@
         if m:
             send_on(m - 1)
     send_on(3)
+    all_r = pltpu.make_async_remote_copy(
+        src_ref=send_r.at[pl.ds(0, 31)], dst_ref=recv_r.at[pl.ds(0, 31)],
+        send_sem=sr, recv_sem=rr, device_id=sibling, device_id_type=MESH,
+    )
+    all_r.wait_recv()
     final = send_r[chip]
     for to in others:
-        pltpu.make_async_remote_copy(
-            src_ref=send_r.at[to], dst_ref=recv_r.at[to], send_sem=sr.at[to], recv_sem=rr.at[to],
-            device_id=(row, to * 2 + core), device_id_type=MESH,
-        ).wait_recv()
         final = final + recv_r[to]
     out_ref[...] = final * scale
-    for to in others:
-        remote(to).wait_send()
-    for c in [*copies_a, pair, *copies_c]:
+    for c in [all_a, all_r, pair, *copies_c]:
         c.wait_send()
 
 
@@ -233,7 +234,7 @@
         in_specs=[hbm] * 6,
         out_specs=pl.BlockSpec(memory_space=pltpu.VMEM),
         scratch_shapes=[
-            pltpu.VMEM((8, 2, 4, 16, 1024), F32),
+            pltpu.VMEM((4, 2, 4, 2, 16, 1024), F32),
             pltpu.VMEM((4, 256, 1024), BF),
             pltpu.VMEM((4, 256, 1024), BF),
             pltpu.VMEM((16, 128), F32),
@@ -255,9 +256,9 @@
             pltpu.VMEM((4, 128, 128), F32),
             pltpu.VMEM((32, 16, 128), F32),
             pltpu.VMEM((32, 16, 128), F32),
-            dma((5,)), dma((8,)),
-            dma((31,)), dma((31,)), dma((1,)), dma((1,)),
-            dma((4,)), dma((4,)), dma((32,)), dma((32,)),
+            dma((5,)), dma((4,)),
+            dma, dma, dma, dma,
+            dma((4,)), dma((4,)), dma, dma,
         ],
         compiler_params=pltpu.CompilerParams(
             collective_id=0, has_side_effects=True, vmem_limit_bytes=40 * 1024 * 1024

time: 32.2 us -> 31 us (0.963)
  Pallas kernels: 31.4 us -> 30.2 us
    pallas_call x1, Pallas kernels: 31.4 us -> 30.2 us  [body(): pl.pallas_call(kernel, out_shape=jax.ShapeDtypeStruct((16, 128), F32), in...]
where the time goes in v4:
time: 31 us; the launch traced here: 30.8 us
  Pallas kernels  30.2 us (97%)
  local copies, waits for them, and re-layouts  0.6 us (2%)
    pallas_call x1, Pallas kernels, body(): pl.pallas_call(kernel, out_shape=jax.ShapeDtypeStruct((16, 128), F32), in...  30.2 us

profile of v4, /device:TPU:1, one launch (start us, length us, event | category | flops | bytes accessed | tf_op | source)
XLA Modules:
  0.0 30.8 jit_solution(18225387325290108184)
XLA Ops:
  0.0 30.2 %top_merge.1 = f32[16,128]{1,0:T(8,128)S(1)} custom-call(f32[8,4,2,16,1024]{4,3,2,1,0:T(8,128)} %bitcast.6, f32[16,128]{1,0:T(8,128)} %bitcast.7, f32[16,128]{1,0:T(8,128)} %bitcast.8, f32[1,128]{1,0:T(1,128)} %bitcast.11, s32[16,128]{1,0:T(8,128)} %bitcast.9, s32[16,128]{1,0:T(8,128)} %bitcast.10), custom_call_target="tpu_custom_call" | custom-call | tf_op jit(solution)/shard_map/top_merge/pallas_call | solution.py:231
  30.2 0.6 %copy.8 = f32[16,128]{1,0:T(8,128)} copy(f32[16,128]{1,0:T(8,128)S(1)} %top_merge.1) | data formatting | bytes 16384

commit v5 on v4

--- a/solution.py
+++ b/solution.py
@@ -29,9 +29,9 @@
 def kernel(
     slab, poles_in, coup_in, roots_in, defl_in, cmap_in, out_ref,
     sf, sh, sl, poles, coup, roots, defl, cmap,
-    pieces, hots, slots, outgoing, recv_a, recv_b, pass_b,
+    pieces, hots, slots, outgoing, recv_a,
     place_l, place_r, entry, prod, recv_c, send_r, recv_r,
-    in_sem, slab_sem, sa, ra, sb, rb, sc, rc, sr, rr,
+    in_sem, slab_sem, sa, ra, sc, rc, sr, rr,
 ):
     row = lax.axis_index("row")
     col = lax.axis_index("col")
@@ -52,13 +52,13 @@
     ]
     for c in smalls:
         c.start()
+    everyone = [to * 2 + c for to in others for c in (core, 1 - core)] + [chip * 2 + (1 - core)]
     barrier = pltpu.get_barrier_semaphore()
-    for to in others:
-        pl.semaphore_signal(barrier, inc=1, device_id=(row, to * 2 + core), device_id_type=MESH)
-    pl.semaphore_signal(barrier, inc=1, device_id=sibling, device_id_type=MESH)
+    for to in everyone:
+        pl.semaphore_signal(barrier, inc=1, device_id=(row, to), device_id_type=MESH)
 
     slabs = [
-        pltpu.make_async_copy(slab.at[pl.ds(2 * i, 2)], sf.at[i], slab_sem.at[i]) for i in range(4)
+        pltpu.make_async_copy(slab.at[:, i], sf.at[i], slab_sem.at[i]) for i in range(4)
     ]
     for c in slabs:
         c.start()
@@ -71,8 +71,7 @@
     within = cm - upper * HALF
     target = within >> 10
     local = within & 1023
-    order = (target & 1) * 32 + (target >> 1)
-    order = jnp.where(upper == row // 4, order, -1)
+    order = jnp.where(upper == row // 4, target, -1)
     pole_v = poles[...]
     coup_v = jnp.where(defl[...] == 0, coup[...], 0.0)
     vals = (
@@ -109,17 +108,17 @@
         e = coup_v[b:b + 1, :] / (pole_v[b:b + 1, :] - roots_t)
         sums = sums + e * e
     sums = jnp.sum(jnp.transpose(sums), axis=0, keepdims=True)
-    low_lane = lax.broadcasted_iota(jnp.int32, (32, 128), 1) < 64
-    for i, v in enumerate((pole_o, coup_o, at_o)):
-        outgoing[i] = jnp.where(low_lane, v[:32], v[32:])
-    outgoing[3] = jnp.broadcast_to(sums, (32, 128))
-
-    pl.semaphore_wait(barrier, 32)
-    for to in others:
+    low_lane = lax.broadcasted_iota(jnp.int32, (64, 128), 1) < 64
+    outgoing[0] = jnp.where(low_lane, pole_o, coup_o)
+    outgoing[1] = at_o
+    outgoing[2] = jnp.broadcast_to(sums, (64, 128))
+
+    pl.semaphore_wait(barrier, 63)
+    for to in everyone:
         c = pltpu.make_async_remote_copy(
-            src_ref=outgoing.at[:, pl.ds(to, 1)], dst_ref=recv_a.at[:, pl.ds(chip, 1)],
+            src_ref=outgoing.at[:, pl.ds(to, 1)], dst_ref=recv_a.at[:, pl.ds(col, 1)],
             send_sem=sa, recv_sem=ra,
-            device_id=(row, to * 2 + core), device_id_type=MESH,
+            device_id=(row, to), device_id_type=MESH,
         )
         c.start()
 
@@ -136,27 +135,18 @@
                 sl[m, at16, :] = (v - hi.astype(F32)).astype(BF)
 
     all_a = pltpu.make_async_remote_copy(
-        src_ref=outgoing.at[:, pl.ds(0, 31)], dst_ref=recv_a.at[:, pl.ds(0, 31)],
+        src_ref=outgoing.at[:, pl.ds(0, 63)], dst_ref=recv_a.at[:, pl.ds(0, 63)],
         send_sem=sa, recv_sem=ra, device_id=sibling, device_id_type=MESH,
     )
     all_a.wait_recv()
-    here = lax.broadcasted_iota(jnp.int32, (32, 128), 0) == chip
-    for i in range(4):
-        v = jnp.where(here, outgoing[i], recv_a[i])
-        pass_b[i] = v if i < 3 else jnp.broadcast_to(jnp.sum(v, axis=0, keepdims=True), (32, 128))
-    pair = pltpu.make_async_remote_copy(
-        src_ref=pass_b, dst_ref=recv_b, send_sem=sb, recv_sem=rb,
-        device_id=sibling, device_id_type=MESH,
-    )
-    pair.start()
-    pair.wait_recv()
-
-    own_lane = (lax.broadcasted_iota(jnp.int32, (32, 128), 1) >> 6) == core
-    pole_r, coup_r, loc_r = (
-        jnp.where(own_lane, pass_b[i], pltpu.roll(recv_b[i], 64, 1)) for i in range(3)
-    )
-    scale = lax.rsqrt(pass_b[3, 0:1, :] + recv_b[3, 0:1, :])
-    loc_r = loc_r.astype(jnp.int32)
+    here = lax.broadcasted_iota(jnp.int32, (64, 128), 0) == col
+    val, loc, sums = (jnp.where(here, outgoing[i], recv_a[i]) for i in range(3))
+    scale = lax.rsqrt(jnp.sum(sums, axis=0, keepdims=True))
+
+    low32 = lax.broadcasted_iota(jnp.int32, (32, 128), 1) < 64
+    pole_r = jnp.where(low32, val[:32], pltpu.roll(val[32:], 64, 1))
+    coup_r = jnp.where(low32, pltpu.roll(val[:32], 64, 1), val[32:])
+    loc_r = jnp.where(low32, loc[:32], pltpu.roll(loc[32:], 64, 1)).astype(jnp.int32)
     loc_h = loc_r >> 7
     loc_l = loc_r & 127
     parts = (*split3(pole_r), *split3(coup_r))
@@ -184,9 +174,11 @@
 
     def send_on(m):
         copies_c[m].wait_recv()
-        send_r[pl.ds(8 * m, 8)] = (prod[m, core] + recv_c[m]).reshape(8, 16, 128)
+        both = (prod[m, core] + recv_c[m]).reshape(8, 16, 128)
+        send_r[pl.ds(4 * m, 4)] = both[:4]
+        send_r[pl.ds(4 * m + 16, 4)] = both[4:]
         for i in range(8):
-            to = (2 * m + i // 4) * 4 + lax.rem(x + STEPS_X[i % 4], 4)
+            to = (m + i // 4 * 4) * 4 + lax.rem(x + STEPS_X[i % 4], 4)
 
             @pl.when(to != chip)
             def _():
@@ -221,7 +213,7 @@
     for to in others:
         final = final + recv_r[to]
     out_ref[...] = final * scale
-    for c in [all_a, all_r, pair, *copies_c]:
+    for c in [all_a, all_r, *copies_c]:
         c.wait_send()
 
 
@@ -245,10 +237,8 @@
             pltpu.VMEM((512, 2048), BF),
             pltpu.VMEM((1024, 128), BF),
             pltpu.VMEM((128, 2048), BF),
-            pltpu.VMEM((4, 32, 128), F32),
-            pltpu.VMEM((4, 32, 128), F32),
-            pltpu.VMEM((4, 32, 128), F32),
-            pltpu.VMEM((4, 32, 128), F32),
+            pltpu.VMEM((3, 64, 128), F32),
+            pltpu.VMEM((3, 64, 128), F32),
             pltpu.VMEM((128, 4096), BF),
             pltpu.VMEM((48, 4096), BF),
             pltpu.VMEM((256, 1024), BF),
@@ -257,7 +247,7 @@
             pltpu.VMEM((32, 16, 128), F32),
             pltpu.VMEM((32, 16, 128), F32),
             dma((5,)), dma((4,)),
-            dma, dma, dma, dma,
+            dma, dma,
             dma((4,)), dma((4,)), dma, dma,
         ],
         compiler_params=pltpu.CompilerParams(
@@ -268,7 +258,7 @@
         *(
             pltpu.with_memory_space_constraint(v, pltpu.HBM)
             for v in (
-                eigen_slab.reshape(8, 4, 2, 16, 1024),
+                eigen_slab.reshape(2, 4, 4, 2, 16, 1024),
                 secular_poles.reshape(16, 128),
                 coupling.reshape(16, 128),
                 window_roots.reshape(1, 128),

time: 31 us -> 30.5 us (0.984)
  the two profiles are of different devices: /device:TPU:1 before, /device:TPU:8 now
where the time goes in v5:
time: 30.5 us; the launch traced here: 30.4 us
  Pallas kernels  29.8 us (98%)
  local copies, waits for them, and re-layouts  0.6 us (2%)
    pallas_call x1, Pallas kernels, body(): pl.pallas_call(kernel, out_shape=jax.ShapeDtypeStruct((16, 128), F32), in...  29.8 us

profile of v5, /device:TPU:8, one launch (start us, length us, event | category | flops | bytes accessed | tf_op | source)
XLA Modules:
  0.0 30.4 jit_solution(6629579677821415988)
XLA Ops:
  0.0 29.8 %top_merge.1 = f32[16,128]{1,0:T(8,128)S(1)} custom-call(f32[2,4,4,2,16,1024]{5,4,3,2,1,0:T(8,128)} %bitcast.6, f32[16,128]{1,0:T(8,128)} %bitcast.7, f32[16,128]{1,0:T(8,128)} %bitcast.8, f32[1,128]{1,0:T(1,128)} %bitcast.11, s32[16,128]{1,0:T(8,128)} %bitcast.9, s32[16,128]{1,0:T(8,128)} %bitcast.10), custom_call_target="tpu_custom_call" | custom-call | tf_op jit(solution)/shard_map/top_merge/pallas_call | solution.py:223
  29.8 0.6 %copy.8 = f32[16,128]{1,0:T(8,128)} copy(f32[16,128]{1,0:T(8,128)S(1)} %top_merge.1) | data formatting | bytes 16384

commit v6 on v5

--- a/solution.py
+++ b/solution.py
@@ -54,7 +54,7 @@
         c.start()
     everyone = [to * 2 + c for to in others for c in (core, 1 - core)] + [chip * 2 + (1 - core)]
     barrier = pltpu.get_barrier_semaphore()
-    for to in everyone:
+    for to in everyone[:36]:
         pl.semaphore_signal(barrier, inc=1, device_id=(row, to), device_id_type=MESH)
 
     slabs = [
@@ -113,6 +113,8 @@
     outgoing[1] = at_o
     outgoing[2] = jnp.broadcast_to(sums, (64, 128))
 
+    for to in everyone[36:]:
+        pl.semaphore_signal(barrier, inc=1, device_id=(row, to), device_id_type=MESH)
     pl.semaphore_wait(barrier, 63)
     for to in everyone:
         c = pltpu.make_async_remote_copy(
@@ -180,9 +182,13 @@
         for i in range(8):
             to = (m + i // 4 * 4) * 4 + lax.rem(x + STEPS_X[i % 4], 4)
 
-            @pl.when(to != chip)
-            def _():
+            if STEPS_X[i % 4]:
                 remote(to).start()
+            else:
+
+                @pl.when(to != chip)
+                def _():
+                    remote(to).start()
 
     def remote(to):
         return pltpu.make_async_remote_copy(

time: 30.5 us -> 30.4 us (level)
  the two profiles are of different devices: /device:TPU:8 before, /device:TPU:120 now
where the time goes in v6:
time: 30.4 us; the launch traced here: 30.2 us
  Pallas kernels  29.6 us (97%)
  local copies, waits for them, and re-layouts  0.6 us (2%)
    pallas_call x1, Pallas kernels, body(): pl.pallas_call(kernel, out_shape=jax.ShapeDtypeStruct((16, 128), F32), in...  29.6 us

profile of v6, /device:TPU:120, one launch (start us, length us, event | category | flops | bytes accessed | tf_op | source)
XLA Modules:
  0.0 30.2 jit_solution(12329047231346714136)
XLA Ops:
  0.0 29.6 %top_merge.1 = f32[16,128]{1,0:T(8,128)S(1)} custom-call(f32[2,4,4,2,16,1024]{5,4,3,2,1,0:T(8,128)} %bitcast.6, f32[16,128]{1,0:T(8,128)} %bitcast.7, f32[16,128]{1,0:T(8,128)} %bitcast.8, f32[1,128]{1,0:T(1,128)} %bitcast.11, s32[16,128]{1,0:T(8,128)} %bitcast.9, s32[16,128]{1,0:T(8,128)} %bitcast.10), custom_call_target="tpu_custom_call" | custom-call | tf_op jit(solution)/shard_map/top_merge/pallas_call | solution.py:229
  29.6 0.6 %copy.8 = f32[16,128]{1,0:T(8,128)} copy(f32[16,128]{1,0:T(8,128)S(1)} %top_merge.1) | data formatting | bytes 16384
